TPU v7x, 32 devices: a whole 2x2x4 slice. The times are simulated.
32 devices in a mesh: segment: 2 (over core), dp: 4 (over y, x), mp: 4 (over z).
Axes of the slice: x: 2, y: 2, z: 4, core: 2. Of those that a mesh axis runs over, the one named last changes fastest.
Arguments:
- queries: bfloat16 [2, 8, 256, 4096], P('segment', 'dp', None, 'mp'), may hold values from -500 to 500
- vision: bfloat16 [8, 48, 8192], P('dp', 'segment'), may hold values from -6 to 6
- w_key: bfloat16 [2, 8192, 512], P('segment', None, 'mp'), may hold values from -0.0625 to 0.0625
- w_value: bfloat16 [2, 8192, 512], P('segment', None, 'mp'), may hold values from -0.0625 to 0.0625
- masks: int32 [8, 2, 2], P('dp'), may hold values 0 or 1
- lengths: int32 [8], P('dp'), may hold values from 1 to 256, as said below
- grad_context: bfloat16 [2, 8, 256, 4096], P('segment', 'dp', None, 'mp'), may hold values from -6 to 6
Outputs:
- context: bfloat16 [2, 8, 256, 4096], P('segment', 'dp', None, 'mp')
- grad_vision: float32 [4, 96, 8192], P('dp', ('segment', 'mp'))
- grad_w_key: float32 [2, 8192, 512], P('segment', 'dp', 'mp')
- grad_w_value: float32 [2, 8192, 512], P('segment', 'dp', 'mp')
Inputs may be any that keep to these rules, and one draw needn't show every extreme that they name: `lengths`: some sample has all 256 positions.
All inputs are finite; a program needn't handle non-finite values. No bound on the sum of `masks` on one device may be relied on, other than what follows from the above.
Results may differ from a plain program's by a relative error of at most 0.011.
Values may be sent and summed in bfloat16 or wider, within the bound.
No kernel may reach another device: no remote copies, remote signals or barrier semaphores. Data moves between devices by JAX's collectives and lax.ppermute only.
A program may use at most 64 MiB of HBM per device.

v0:
```python
import math

import jax
import jax.numpy as jnp
from jax import lax
from jax.sharding import PartitionSpec as P

D = 8192
HD = 128
TB = 128
TILE_TOK = 24


EPSILON = 1e-06


def normalize(values_in):
    factor = lax.rsqrt(jnp.mean(values_in * values_in, axis=-1, keepdims=True) + EPSILON)
    return (values_in * factor, factor)


def per_device(queries, vision, w_key, w_value, masks, lengths, grad_context):
    gathered = lax.all_gather(vision, "segment", axis=1, tiled=True)
    samples = gathered.shape[0]
    tile_rows = gathered.shape[1]
    flat_rows = samples * tile_rows
    flat_vision = gathered.reshape(flat_rows, D)
    weight_pair = jnp.concatenate([w_key[0], w_value[0]], axis=1)
    projected = jnp.dot(flat_vision, weight_pair, preferred_element_type=jnp.float32)
    key_norm, key_factor = normalize(projected[:, :HD])
    key_rows = key_norm.astype(jnp.bfloat16).reshape(samples, tile_rows, HD)
    value_rows = projected[:, HD:].astype(jnp.bfloat16).reshape(samples, tile_rows, HD)
    head_count = queries.shape[3] // HD
    text_rows = queries.shape[2]
    query_raw = queries[0].astype(jnp.float32).reshape(samples, text_rows, head_count, HD)
    query_rows = normalize(query_raw)[0].astype(jnp.bfloat16)
    spread = jnp.broadcast_to(
        masks[:, :, None, :, None], (samples, masks.shape[1], TB, masks.shape[2], TILE_TOK)
    )
    spread = spread.reshape(samples, text_rows, tile_rows)
    position = jnp.arange(text_rows, dtype=jnp.int32)
    allowed = jnp.where(
        (spread == 1) & (position[None, :, None] < lengths[:, None, None]), 1.0, 0.0
    ).astype(jnp.float32)
    root_scale = 1.0 / math.sqrt(HD)
    scores = (
        jnp.einsum("bthd,bjd->bhtj", query_rows, key_rows, preferred_element_type=jnp.float32)
        * root_scale
    )
    exponent = jnp.exp(scores) * allowed[:, None]
    denominator = jnp.sum(exponent, axis=-1, keepdims=True)
    probability = exponent / jnp.where(denominator > 0, denominator, 1.0)
    weights = probability.astype(jnp.bfloat16)
    context = jnp.einsum("bhtj,bjd->bthd", weights, value_rows, preferred_element_type=jnp.float32)
    context = context.astype(jnp.bfloat16).reshape(1, samples, text_rows, head_count * HD)
    grad_rows = grad_context[0].reshape(samples, text_rows, head_count, HD)
    grad_weights = jnp.einsum(
        "bthd,bjd->bhtj", grad_rows, value_rows, preferred_element_type=jnp.float32
    )
    grad_scores = (
        probability
        * (grad_weights - jnp.sum(probability * grad_weights, axis=-1, keepdims=True))
        * root_scale
    )
    grad_scores = grad_scores.astype(jnp.bfloat16)
    grad_key_norm = jnp.einsum(
        "bhtj,bthd->bjd", grad_scores, query_rows, preferred_element_type=jnp.float32
    )
    grad_key_norm = grad_key_norm.reshape(flat_rows, HD)
    grad_keys = key_factor * (
        grad_key_norm - key_norm * jnp.mean(grad_key_norm * key_norm, axis=-1, keepdims=True)
    )
    grad_values = jnp.einsum(
        "bhtj,bthd->bjd", weights, grad_rows, preferred_element_type=jnp.float32
    )
    grad_values = grad_values.reshape(flat_rows, HD)
    pair_grads = jnp.concatenate(
        [grad_keys.astype(jnp.bfloat16), grad_values.astype(jnp.bfloat16)], axis=1
    )
    partial_sum = lax.dot_general(
        pair_grads, weight_pair, (((1,), (1,)), ((), ())), preferred_element_type=jnp.float32
    )
    vision_sum = lax.psum_scatter(partial_sum, ("segment", "mp"), scatter_dimension=0, tiled=True)
    grad_vision = vision_sum.reshape(1, vision_sum.shape[0], D)
    summed = lax.psum_scatter(
        lax.dot_general(
            flat_vision, pair_grads, (((0,), (0,)), ((), ())), preferred_element_type=jnp.float32
        ).astype(jnp.bfloat16),
        "dp",
        scatter_dimension=0,
        tiled=True,
    ).astype(jnp.float32)
    grad_w_key = summed[:, :HD].reshape(1, summed.shape[0], HD)
    grad_w_value = summed[:, HD:].reshape(1, summed.shape[0], HD)
    return (context, grad_vision, grad_w_key, grad_w_value)


def solution(mesh):
    in_specs = (
        P("segment", "dp", None, "mp"),
        P("dp", "segment", None),
        P("segment", None, "mp"),
        P("segment", None, "mp"),
        P("dp", None, None),
        P("dp"),
        P("segment", "dp", None, "mp"),
    )
    out_specs = (
        P("segment", "dp", None, "mp"),
        P("dp", ("segment", "mp"), None),
        P("segment", "dp", "mp"),
        P("segment", "dp", "mp"),
    )
    return jax.shard_map(
        per_device, mesh=mesh, in_specs=in_specs, out_specs=out_specs, check_vma=False
    )
```

profile of v0, /device:TPU:24, one launch (start us, length us, event | category | flops | bytes accessed | tf_op | source)
XLA Modules:
  0.0 175.1 jit_solution(4624681457793615070)
XLA Ops:
  7.2 0.7 all-gather.2.cloned.1.call-update
  7.9 1.5 copy.51
  9.5 0.6 fusion.5
  10.2 0.1 copy.37
  10.4 0.1 copy.39
  10.6 1.5 copy.52
  12.2 1.5 fusion.6
  13.7 6.9 %all-gather.2.cloned.1.call-done = bf16[2,48,8192]{2,1,0:T(8,128)(2,1)} async-done(((bf16[2,24,8192]{2,1,0:T(8,128)(2,1)}), bf16[2,48,8192]{2,1,0:T(8,128)(2,1)}) %all-gather.2.cloned.1.call-update) | async-done | bytes 1572880 | tf_op jit(solution)/shard_map/all_gather | solution.py:23
  20.6 3.6 %fusion.15 = f32[96,256]{1,0:T(8,128)S(1)} fusion(bf16[96,8192]{1,0:T(8,128)(2,1)} %bitcast.87, bf16[8192,128]{1,0:T(8,128)(2,1)} %bitcast.83, bf16[8192,128]{1,0:T(8,128)(2,1)} %bitcast.85), kind=kOutput, calls=%fused_computation.21 | convolution fusion | flops 411041792 | bytes 5865472 | tf_op jit(solution)/shard_map/dot_general | solution.py:29
  24.2 0.1 multiply_reduce_fusion.1
  24.4 0.5 fusion.35
  24.9 0.5 convolution_bitcast_fusion
  25.4 0.4 copy-done.2
  25.8 0.3 fusion.16
  26.1 1.9 %fusion.14 = f32[2,48,128,1]{2,1,3,0:T(8,128)S(1)} fusion(f32[2,8,256,48]{2,3,1,0:T(8,128)S(1)} %convolution_bitcast_fusion, bf16[2,256,8,128]{3,2,1,0:T(8,128)(2,1)S(1)} %copy-done.1, f32[2,8,256,48]{2,3,1,0:T(8,128)} %copy-done.2, f32[2,8,256]{2,1,0:T(8,128)S(1)} %compare_select_fusion), kind=kOutput, calls=%fused_computation.20 | convolution fusion | flops 51712048 | bytes 2686976 | tf_op jit(solution)/shard_map/bhtj,bthd->bjd/dot_general | solution.py:66
  28.0 0.2 fusion.26
  28.3 4.6 %fusion.2 = bf16[8192,256]{0,1:T(8,128)(2,1)} fusion(bf16[96,8192]{1,0:T(8,128)(2,1)} %bitcast.88, bf16[96,128]{1,0:T(8,128)(2,1)S(1)} %bitcast.92, bf16[96,128]{1,0:T(8,128)(2,1)S(1)} %fusion.28), kind=kOutput, calls=%fused_computation.2 | convolution fusion | flops 404848640 | bytes 5816320 | tf_op jit(solution)/shard_map/dot_general | solution.py:86
  33.0 3.6 %fusion.3 = f32[96,8192]{1,0:T(8,128)S(1)} fusion(bf16[8192,128]{1,0:T(8,128)(2,1)} %bitcast.84, bf16[8192,128]{1,0:T(8,128)(2,1)} %bitcast.86, bf16[96,128]{1,0:T(8,128)(2,1)S(1)} %bitcast.93, bf16[96,128]{1,0:T(8,128)(2,1)S(1)} %fusion.28), kind=kOutput, calls=%fused_computation.4 | convolution fusion | flops 411140096 | bytes 7389184 | tf_op jit(solution)/shard_map/dot_general | solution.py:80
  36.6 84.9 %fusion = f32[16,8192]{1,0:T(8,128)} fusion(f32[96,8192]{1,0:T(8,128)S(1)} %fusion.3), kind=kCustom, calls=%all-reduce-scatter | all-reduce-scatter fusion | flops 1048577 | bytes 3670528
  121.5 5.9 %collective-permute-start = (f32[16,8192]{1,0:T(8,128)}, f32[16,8192]{1,0:T(8,128)S(1)}, u32[]{:S(2)}, u32[]{:S(2)}) collective-permute-start(f32[16,8192]{1,0:T(8,128)} %fusion), channel_id=1, source_target_pairs={{0,1},{1,2},{2,3},{3,16},{16,17},{17,18},{18,19},{4,5},{5,6},{6,7}... | collective-permute-start | bytes 1572872
  127.4 1.1 slice.21
  128.5 1.9 %collective-permute-start.1 = (f32[12,8192]{1,0:T(8,128)S(1)}, f32[12,8192]{1,0:T(8,128)S(1)}, u32[]{:S(2)}, u32[]{:S(2)}) collective-permute-start(f32[12,8192]{1,0:T(8,128)S(1)} %slice.21), channel_id=1, source_target_pairs={{0,2},{1,3},{2,16},{3,17},{16,18},{17,19},{4,6},{5,7},{6,20},{7,21... | collective-permute-start | bytes 1179656
  130.4 0.6 dynamic-slice.4
  131.7 1.7 convolution_convert_fusion.1
  133.3 1.3 copy.43
  134.6 26.8 %collective-permute-done.1 = f32[12,8192]{1,0:T(8,128)S(1)} collective-permute-done((f32[12,8192]{1,0:T(8,128)S(1)}, f32[12,8192]{1,0:T(8,128)S(1)}, u32[]{:S(2)}, u32[]{:S(2)}) %collective-permute-start.1) | collective-permute-done | bytes 393248
  161.4 1.3 concatenate.8
  162.8 1.2 copy.44
  163.9 1.5 convert_element_type.61
  165.4 0.2 slice_bitcast_fusion
  165.6 1.3 copy.45
  166.9 1.3 copy.46
  (30 shorter events, 0.8 us)
Async XLA Ops:
  7.2 13.4 %all-gather.2.cloned.1.call-start = ((), (), s32[]{:S(2)}) async-start(), calls=%async_computation.1 | async-start | bytes 2359296 | tf_op jit(solution)/shard_map/all_gather | solution.py:23
  7.9 156.0 %reduce-scatter.4.cloned.1.call-start = ((), (), s32[]{:S(2)}) async-start(), calls=%async_computation.2 | async-start | bytes 5242880 | tf_op jit(solution)/shard_map/reduce_scatter | solution.py:85
  9.4 0.9 copy-start.3
  9.4 2.7 %copy-start.5 = (s32[2]{0:T(128)S(1)}, s32[2]{0:T(128)}, u32[]{:S(2)}) copy-start(s32[2]{0:T(128)} %param.12) | copy-start | bytes 28
  20.6 3.8 %copy-start.1 = (bf16[2,256,8,128]{3,2,1,0:T(8,128)(2,1)S(1)}, bf16[2,256,8,128]{3,2,1,0:T(8,128)(2,1)}, u32[]{:S(2)}) copy-start(bf16[2,256,8,128]{3,2,1,0:T(8,128)(2,1)} %fusion.6) | copy-start | bytes 3145732
  24.9 0.9 copy-start.2
  36.6 93.8 %copy-start.4 = (u32[32]{0:T(128)S(1)}, u32[32]{0:T(128)}, u32[]{:S(2)}) copy-start(u32[32]{0:T(128)} %constant.27) | copy-start | bytes 388
  121.5 39.9 %collective-permute-start = (f32[16,8192]{1,0:T(8,128)}, f32[16,8192]{1,0:T(8,128)S(1)}, u32[]{:S(2)}, u32[]{:S(2)}) collective-permute-start(f32[16,8192]{1,0:T(8,128)} %fusion), channel_id=1, source_target_pairs={{0,1},{1,2},{2,3},{3,16},{16,17},{17,18},{18,19},{4,5},{5,6},{6,7}... | collective-permute-start | bytes 1572872
  128.5 32.9 %collective-permute-start.1 = (f32[12,8192]{1,0:T(8,128)S(1)}, f32[12,8192]{1,0:T(8,128)S(1)}, u32[]{:S(2)}, u32[]{:S(2)}) collective-permute-start(f32[12,8192]{1,0:T(8,128)S(1)} %slice.21), channel_id=1, source_target_pairs={{0,2},{1,3},{2,16},{3,17},{16,18},{17,19},{4,6},{5,7},{6,20},{7,21... | collective-permute-start | bytes 1179656
  131.7 29.8 %copy-start = (f32[16,8192]{1,0:T(8,128)S(1)}, f32[16,8192]{1,0:T(8,128)}, u32[]{:S(2)}) copy-start(f32[16,8192]{1,0:T(8,128)} %fusion) | copy-start | bytes 1572868
Sparse Core Ops, SparseCore 0:
  9.5 11.0 all-gather.1
  33.1 53.4 reduce-scatter.3
where the time goes:
time: 176 us; the launch traced here: 175 us
  blocking collectives  84.9 us (48%)
  waiting for transfers between devices  34.3 us (19%)
  matrix products  16.6 us (9%)
  between operations  15 us (9%)
  local copies, waits for them, and re-layouts  12.2 us (7%)
  starting transfers between devices  7.89 us (4%)
  other arithmetic  4.14 us (2%)
    unnamed x1, blocking collectives  84.9 us
    unnamed x4, waiting for transfers between devices  27.5 us
    unnamed x21, local copies, waits for them, and re-layouts  11.4 us
    unnamed x2, starting transfers between devices  7.81 us
    all_gather x1, waiting for transfers between devices, per_device(): gathered = lax.all_gather(vision, 'segment', axis=1, tiled=True)  6.85 us
    dot_general x1, matrix products, per_device(): lax.dot_general(flat_vision, pair_grads, (((0,), (0,)), ((), ())), prefer...  4.61 us
    dot_general x1, matrix products, per_device(): lax.dot_general(pair_grads, weight_pair, (((1,), (1,)), ((), ())), prefer...  3.61 us
    dot_general x1, matrix products, per_device(): jnp.dot(flat_vision, weight_pair, preferred_element_type=jnp.float32)  3.58 us
  transfers between devices with their start and end apart: 4, of which 2 were waited for; matrix products, arithmetic and copies ran while one was open for 58% of the time, Pallas kernels for 0%

commit v1 on v0

v1 whole, which is shorter than its diff:
```python
import math

import jax
import jax.numpy as jnp
from jax import lax
from jax.sharding import PartitionSpec as P

EPSILON = 1e-06
F32 = jnp.float32
BF16 = jnp.bfloat16


def normalize(values_in):
    factor = lax.rsqrt(jnp.mean(values_in * values_in, axis=-1, keepdims=True) + EPSILON)
    return (values_in * factor, factor)


def partner(index, step, size):
    if size & (size - 1) == 0:
        return index ^ step
    return (index + step) % size


def source(index, step, size):
    if size & (size - 1) == 0:
        return index ^ step
    return (index - step) % size


def swap(value, axis, step, size):
    return lax.ppermute(value, axis, [(i, partner(i, step, size)) for i in range(size)])


def block_of(value, index, size, axis):
    return lax.dynamic_slice_in_dim(value, index * size, size, axis)


def build(mesh):
    n_seg, n_dp, n_mp = (mesh.shape[name] for name in ("segment", "dp", "mp"))

    def per_device(queries, vision, w_key, w_value, masks, lengths, grad_context):
        seg, dp, mp = (lax.axis_index(name) for name in ("segment", "dp", "mp"))
        samples, part, width = vision.shape
        tile_rows = part * n_seg
        rows = samples * tile_rows
        hd = w_key.shape[2]
        own = vision.reshape(samples * part, width)
        parts = [own] + [swap(own, "segment", r, n_seg) for r in range(1, n_seg)]
        columns = width // n_dp
        slices = [block_of(own, dp, columns, 1)]
        for k in range(1, n_dp):
            slices.append(swap(block_of(own, partner(dp, k, n_dp), columns, 1), "dp", k, n_dp))
        slices = jnp.concatenate(slices, axis=0)
        columns_of = [slices] + [swap(slices, "segment", r, n_seg) for r in range(1, n_seg)]

        weight_pair = jnp.concatenate([w_key[0], w_value[0]], axis=1)
        projected = jnp.zeros((samples, tile_rows, 2 * hd), F32)
        for r, piece in enumerate(parts):
            product = jnp.dot(piece, weight_pair, preferred_element_type=F32)
            projected = lax.dynamic_update_slice_in_dim(
                projected, product.reshape(samples, part, 2 * hd), source(seg, r, n_seg) * part, 1
            )
        projected = projected.reshape(rows, 2 * hd)
        key_norm, key_factor = normalize(projected[:, :hd])
        key_rows = key_norm.astype(BF16).reshape(samples, tile_rows, hd)
        value_rows = projected[:, hd:].astype(BF16).reshape(samples, tile_rows, hd)
        head_count = queries.shape[3] // hd
        text_rows = queries.shape[2]
        query_raw = queries[0].astype(F32).reshape(samples, text_rows, head_count, hd)
        query_rows = normalize(query_raw)[0].astype(BF16)
        spread = jnp.broadcast_to(
            masks[:, :, None, :, None],
            (
                samples,
                masks.shape[1],
                text_rows // masks.shape[1],
                masks.shape[2],
                tile_rows // masks.shape[2],
            ),
        ).reshape(samples, text_rows, tile_rows)
        position = jnp.arange(text_rows, dtype=jnp.int32)
        allowed = jnp.where(
            (spread == 1) & (position[None, :, None] < lengths[:, None, None]), 1.0, 0.0
        ).astype(F32)
        root_scale = 1.0 / math.sqrt(hd)
        scores = (
            jnp.einsum("bthd,bjd->bhtj", query_rows, key_rows, preferred_element_type=F32)
            * root_scale
        )
        exponent = jnp.exp(scores) * allowed[:, None]
        denominator = jnp.sum(exponent, axis=-1, keepdims=True)
        probability = exponent / jnp.where(denominator > 0, denominator, 1.0)
        weights = probability.astype(BF16)
        context = jnp.einsum("bhtj,bjd->bthd", weights, value_rows, preferred_element_type=F32)
        context = context.astype(BF16).reshape(1, samples, text_rows, head_count * hd)
        grad_rows = grad_context[0].reshape(samples, text_rows, head_count, hd)
        grad_weights = jnp.einsum("bthd,bjd->bhtj", grad_rows, value_rows, preferred_element_type=F32)
        grad_scores = (
            probability
            * (grad_weights - jnp.sum(probability * grad_weights, axis=-1, keepdims=True))
            * root_scale
        ).astype(BF16)
        grad_key_norm = jnp.einsum(
            "bhtj,bthd->bjd", grad_scores, query_rows, preferred_element_type=F32
        ).reshape(rows, hd)
        grad_keys = key_factor * (
            grad_key_norm - key_norm * jnp.mean(grad_key_norm * key_norm, axis=-1, keepdims=True)
        )
        grad_values = jnp.einsum(
            "bhtj,bthd->bjd", weights, grad_rows, preferred_element_type=F32
        ).reshape(rows, hd)
        pair_grads = jnp.concatenate([grad_keys.astype(BF16), grad_values.astype(BF16)], axis=1)

        def vision_rows(segment):
            return lax.dot_general(
                block_of(pair_grads, segment, rows // n_seg, 0),
                weight_pair,
                (((1,), (1,)), ((), ())),
                preferred_element_type=F32,
            )

        away = [
            swap(vision_rows(partner(seg, r, n_seg)).astype(BF16), "segment", r, n_seg)
            for r in range(1, n_seg)
        ]
        total = vision_rows(seg)
        for piece in away:
            total = total + piece.astype(F32)
        out_rows = rows // (n_seg * n_mp)
        fold = 16 // math.gcd(out_rows, 16)
        folded = total.astype(BF16).reshape(n_mp, out_rows * fold, width // fold)
        kept = lax.dynamic_index_in_dim(total.reshape(n_mp, out_rows, width), mp, 0, keepdims=False)
        for k in reversed(range(1, n_mp)):
            sent = lax.dynamic_index_in_dim(folded, partner(mp, k, n_mp), 0, keepdims=False)
            kept = kept + swap(sent, "mp", k, n_mp).astype(F32).reshape(out_rows, width)
        grad_vision = kept.reshape(1, out_rows, width)

        by_part = pair_grads.reshape(samples, n_seg, part, 2 * hd)
        ordered = jnp.stack(
            [
                lax.dynamic_index_in_dim(by_part, source(seg, r, n_seg), 1, keepdims=False)
                for r in range(n_seg)
            ]
        ).reshape(n_seg, samples * part, 2 * hd)
        groups = jnp.stack(
            [ordered] + [swap(ordered, "dp", k, n_dp) for k in range(1, n_dp)], axis=1
        )
        grad_w = lax.dot_general(
            jnp.concatenate(columns_of, axis=0),
            groups.reshape(n_seg * n_dp * samples * part, 2 * hd),
            (((0,), (0,)), ((), ())),
            preferred_element_type=F32,
        )
        return (context, grad_vision, grad_w[None, :, :hd], grad_w[None, :, hd:])

    return per_device


def solution(mesh):
    in_specs = (
        P("segment", "dp", None, "mp"),
        P("dp", "segment", None),
        P("segment", None, "mp"),
        P("segment", None, "mp"),
        P("dp", None, None),
        P("dp"),
        P("segment", "dp", None, "mp"),
    )
    out_specs = (
        P("segment", "dp", None, "mp"),
        P("dp", ("segment", "mp"), None),
        P("segment", "dp", "mp"),
        P("segment", "dp", "mp"),
    )
    return jax.shard_map(
        build(mesh), mesh=mesh, in_specs=in_specs, out_specs=out_specs, check_vma=False
    )
```

time: 176 us -> 77.1 us (0.44)
  the two profiles are of different devices: /device:TPU:24 before, /device:TPU:0 now
where the time goes in v1:
time: 77.1 us; the launch traced here: 76.5 us
  local copies, waits for them, and re-layouts  24 us (31%)
  matrix products  20.2 us (26%)
  starting transfers between devices  12.7 us (16%)
  waiting for transfers between devices  11.2 us (15%)
  other arithmetic  7.4 us (10%)
  between operations  0.99 us (1%)
    ppermute x12, starting transfers between devices, swap(): lax.ppermute(value, axis, [(i, partner(i, step, size)) for i in range(siz...  12.7 us
    unnamed x25, local copies, waits for them, and re-layouts  11.4 us
    ppermute x12, waiting for transfers between devices, swap(): lax.ppermute(value, axis, [(i, partner(i, step, size)) for i in range(siz...  11.2 us
    dot_general x2, matrix products, vision_rows(): lax.dot_general(block_of(pair_grads, segment, rows // n_seg, 0), weight_p...  8.1 us
    dot_general x2, matrix products, per_device(): product = jnp.dot(piece, weight_pair, preferred_element_type=F32)  6.11 us
    reshape x3, local copies, waits for them, and re-layouts, per_device(): kept = kept + swap(sent, 'mp', k, n_mp).astype(F32).reshape(out_rows, width)  3.05 us
    dot_general x1, matrix products, per_device(): lax.dot_general(jnp.concatenate(columns_of, axis=0), groups.reshape(n_seg...  2.3 us
    concatenate x1, other arithmetic, per_device(): slices = jnp.concatenate(slices, axis=0)  2.18 us
  transfers between devices with their start and end apart: 12, of which 3 were waited for; matrix products, arithmetic and copies ran while one was open for 52% of the time, Pallas kernels for 0%

profile of v1, /device:TPU:0, one launch (start us, length us, event | category | flops | bytes accessed | tf_op | source)
XLA Modules:
  0.0 76.5 jit_solution(14169157366907818450)
XLA Ops:
  1.2 2.2 %constant_dynamic-slice_fusion.2 = (bf16[48,2048]{1,0:T(8,128)(2,1)}, bf16[48,2048]{1,0:T(8,128)(2,1)}, bf16[48,2048]{1,0:T(8,128)(2,1)}, bf16[384,2048]{1,0:T(8,128)(2,1)}, bf16[48,2048]{1,0:T(8,128)(2,1)}) fusion(bf16[48,8192]{1,0:T(8,128)(2,1)} %bitcast.122, s32[]{:T(128)S(6)} %select_n.75, s32[]{:T(128)S(6)} %select_n.74, s32[]{:T(128)S(6)} %select_n.73, ...), kind=kLoop, calls=%fused_computation.67 | loop fusion | bytes 1769488 | tf_op jit(solution)/shard_map/dynamic_slice | solution.py:35
  3.4 2.6 %collective-permute-start.5 = (bf16[48,2048]{1,0:T(8,128)(2,1)}, bf16[48,2048]{1,0:T(8,128)(2,1)}, u32[]{:S(2)}, u32[]{:S(2)}) collective-permute-start(bf16[48,2048]{1,0:T(8,128)(2,1)} %get-tuple-element.30), channel_id=1, source_target_pairs={{0,4},{4,0},{8,12},{12,8},{1,5},{5,1},{9,13},{13,9},{2,6},{6,2},{1... | collective-permute-start | bytes 589832 | tf_op jit(solution)/shard_map/ppermute | solution.py:31
  5.9 1.5 %collective-permute-start.6 = (bf16[48,2048]{1,0:T(8,128)(2,1)}, bf16[48,2048]{1,0:T(8,128)(2,1)}, u32[]{:S(2)}, u32[]{:S(2)}) collective-permute-start(bf16[48,2048]{1,0:T(8,128)(2,1)} %get-tuple-element.29), channel_id=1, source_target_pairs={{0,8},{4,12},{8,0},{12,4},{1,9},{5,13},{9,1},{13,5},{2,10},{6,14},... | collective-permute-start | bytes 589832 | tf_op jit(solution)/shard_map/ppermute | solution.py:31
  10.3 1.6 %copy.65 = bf16[64,8,8,128]{3,2,1,0:T(8,128)(2,1)S(1)} copy(bf16[64,8,8,128]{3,1,2,0:T(8,128)(2,1)} %bitcast.113) | data formatting | bytes 2097152
  12.2 2.7 %fusion.38 = f32[256,48]{0,1:T(8,128)S(1)} fusion(bf16[48,8192]{1,0:T(8,128)(2,1)} %bitcast.123, bf16[8192,128]{1,0:T(8,128)(2,1)S(1)} %bitcast.106, bf16[8192,128]{1,0:T(8,128)(2,1)} %bitcast.108), kind=kOutput, calls=%fused_computation.83 | convolution fusion | flops 209715200 | bytes 5029888 | tf_op jit(solution)/shard_map/dot_general | solution.py:59
  15.0 1.5 %fusion.2 = bf16[2,256,8,128]{3,2,1,0:T(8,128)(2,1)} fusion(f32[2,256,8]{2,1,0:T(8,128)S(1)} %copy.49, f32[2,256,8,128]{3,2,1,0:T(8,128)S(1)} %bitcast.101), kind=kLoop, calls=%fused_computation.6 | loop fusion | flops 1048576 | bytes 3162112 | tf_op jit(solution)/shard_map/convert_element_type | solution.py:70
  17.4 2.2 %pad_maximum_fusion.1 = bf16[192,2048]{1,0:T(8,128)(2,1)} fusion(bf16[48,2048]{1,0:T(8,128)(2,1)} %collective-permute-done.7, bf16[48,2048]{1,0:T(8,128)(2,1)} %collective-permute-done.6, bf16[48,2048]{1,0:T(8,128)(2,1)} %collective-permute-done.5, bf16[48,2048]{1,0:T(8,128)(2,1)} %get-tuple-element.32), kind=kLoop, calls=%fused_computation.27 | loop fusion | flops 3145728 | bytes 1572864 | tf_op jit(solution)/shard_map/concatenate | solution.py:53
  19.6 1.6 %constant_dynamic-update-slice_fusion.3 = bf16[384,2048]{1,0:T(8,128)(2,1)} fusion(bf16[384,2048]{1,0:T(8,128)(2,1)} %get-tuple-element.31, bf16[48,2048]{1,0:T(8,128)(2,1)} %collective-permute-done.5), kind=kLoop, calls=%fused_computation.63 | loop fusion | bytes 393216
  21.2 1.6 %constant_dynamic-update-slice_fusion.2 = bf16[384,2048]{1,0:T(8,128)(2,1)} fusion(bf16[384,2048]{1,0:T(8,128)(2,1)} %constant_dynamic-update-slice_fusion.3, bf16[48,2048]{1,0:T(8,128)(2,1)} %collective-permute-done.6), kind=kLoop, calls=%fused_computation.62 | loop fusion | bytes 393216
  22.8 1.6 %constant_dynamic-update-slice_fusion.1 = bf16[384,2048]{1,0:T(8,128)(2,1)} fusion(bf16[384,2048]{1,0:T(8,128)(2,1)} %constant_dynamic-update-slice_fusion.2, bf16[48,2048]{1,0:T(8,128)(2,1)} %collective-permute-done.7), kind=kLoop, calls=%fused_computation.61 | loop fusion | bytes 393216
  24.4 3.4 %fusion.39 = f32[256,48]{0,1:T(8,128)S(1)} fusion(bf16[48,8192]{1,0:T(8,128)(2,1)} %collective-permute-done, bf16[8192,128]{1,0:T(8,128)(2,1)} %bitcast.104, bf16[8192,128]{1,0:T(8,128)(2,1)} %bitcast.109), kind=kOutput, calls=%fused_computation.84 | convolution fusion | flops 209715200 | bytes 5029888 | tf_op jit(solution)/shard_map/dot_general | solution.py:59
  29.8 1.9 %fusion.10 = f32[2,48,128,1]{2,1,3,0:T(8,128)S(1)} fusion(f32[2,8,256,48]{2,3,1,0:T(8,128)S(1)} %convolution_bitcast_fusion, bf16[2,256,8,128]{3,2,1,0:T(8,128)(2,1)S(1)} %copy-done.2, f32[2,8,256,48]{2,3,1,0:T(8,128)} %copy-done.7, f32[2,8,256]{2,1,0:T(8,128)S(1)} %compare_select_fusion), kind=kOutput, calls=%fused_computation.18 | convolution fusion | flops 51712048 | bytes 2686976 | tf_op jit(solution)/shard_map/bhtj,bthd->bjd/dot_general | solution.py:103
  32.1 2.1 %collective-permute-start.11 = (bf16[2,48,256]{2,1,0:T(8,128)(2,1)S(1)}, bf16[2,48,256]{2,1,0:T(8,128)(2,1)S(1)}, u32[]{:S(2)}, u32[]{:S(2)}) collective-permute-start(bf16[2,48,256]{2,1,0:T(8,128)(2,1)S(1)} %pad_maximum_fusion.4), channel_id=1, source_target_pairs={{0,12},{4,8},{8,4},{12,0},{1,13},{5,9},{9,5},{13,1},{2,14},{6,10},... | collective-permute-start | bytes 147464 | tf_op jit(solution)/shard_map/ppermute | solution.py:31
  35.6 4.4 %convolution_convert_fusion = bf16[48,8192]{1,0:T(8,128)(2,1)} fusion(s32[]{:T(128)S(6)} %select_n.67, bf16[96,128]{1,0:T(8,128)(2,1)S(1)} %fusion.23, bf16[96,128]{1,0:T(8,128)(2,1)S(1)} %bitcast.133, bf16[8192,128]{1,0:T(8,128)(2,1)} %bitcast.105, bf16[8192,128]{1,0:T(8,128)(2,1)} %bitcast.110), kind=kOutput, calls=%fused_computation.1 | convolution fusion | flops 210157568 | bytes 5029892 | tf_op jit(solution)/shard_map/dot_general | solution.py:115
  40.5 1.3 %copy.58 = bf16[1,2,256,1024]{3,2,1,0:T(8,128)(2,1)} copy(bf16[1,2,256,1024]{2,3,1,0:T(8,128)(2,1)S(1)} %bitcast.114) | data formatting | bytes 2097152
  41.9 1.2 %constant_dynamic-update-slice_fusion = bf16[384,2048]{1,0:T(8,128)(2,1)S(1)} fusion(bf16[384,2048]{1,0:T(8,128)(2,1)S(1)} %copy-done, bf16[192,2048]{1,0:T(8,128)(2,1)} %collective-permute-done.8), kind=kLoop, calls=%fused_computation.60 | loop fusion | bytes 1572864 | tf_op jit(solution)/shard_map/concatenate | solution.py:149
  43.1 1.2 %copy-done.1 = bf16[384,2048]{1,0:T(8,128)(2,1)} copy-done((bf16[384,2048]{1,0:T(8,128)(2,1)}, bf16[384,2048]{1,0:T(8,128)(2,1)S(1)}, u32[]{:S(2)}) %copy-start.1) | copy-done | bytes 1572888
  44.3 2.3 %fusion.42 = f32[2048,256]{1,0:T(8,128)S(1)} fusion(bf16[384,2048]{1,0:T(8,128)(2,1)} %copy-done.1, bf16[384,256]{1,0:T(8,128)(2,1)S(1)} %bitcast.120), kind=kOutput, calls=%fused_computation.87 | convolution fusion | flops 402653184 | bytes 3866624 | tf_op jit(solution)/shard_map/dot_general | solution.py:148
  47.0 3.7 %fusion.41 = (bf16[48,8192]{1,0:T(8,128)(2,1)S(1)}, f32[48,8192]{1,0:T(8,128)}) fusion(bf16[48,8192]{1,0:T(8,128)(2,1)} %collective-permute-done.1, bf16[8192,128]{1,0:T(8,128)(2,1)S(1)} %bitcast.107, bf16[8192,128]{1,0:T(8,128)(2,1)S(1)} %bitcast.111, s32[]{:T(128)S(6)} %select_n.66, bf16[96,128]{1,0:T(8,128)(2,1)S(1)} %fusion.23, ...), kind=kOutput, calls=%fused_computation.86 | convolution fusion | flops 210944000 | bytes 7389188 | tf_op jit(solution)/shard_map/dot_general | solution.py:115
  50.6 1.5 %reshape.155 = bf16[4,48,2048]{2,1,0:T(8,128)(2,1)} reshape(bf16[48,8192]{1,0:T(8,128)(2,1)S(1)} %get-tuple-element.40) | data formatting | bytes 1572864 | tf_op jit(solution)/shard_map/reshape | solution.py:131
  52.1 1.2 %dynamic-slice_bitcast_fusion.2 = (bf16[48,2048]{1,0:T(8,128)(2,1)S(1)}, bf16[48,2048]{1,0:T(8,128)(2,1)S(1)}, bf16[48,2048]{1,0:T(8,128)(2,1)S(1)}) fusion(bf16[4,48,2048]{2,1,0:T(8,128)(2,1)} %reshape.155, s32[]{:T(128)S(6)} %select_n.69, s32[]{:T(128)S(6)} %select_n.71, s32[]{:T(128)S(6)} %select_n.70), kind=kLoop, calls=%fused_computation.36 | loop fusion | bytes 1179660 | tf_op jit(solution)/shard_map/jit(dynamic_index_in_dim)/squeeze | solution.py:134
  53.3 1.6 %collective-permute-start.4 = (bf16[48,2048]{1,0:T(8,128)(2,1)S(1)}, bf16[48,2048]{1,0:T(8,128)(2,1)}, u32[]{:S(2)}, u32[]{:S(2)}) collective-permute-start(bf16[48,2048]{1,0:T(8,128)(2,1)S(1)} %get-tuple-element.34), channel_id=1, source_target_pairs={{0,1},{1,0},{2,3},{3,2},{4,5},{5,4},{6,7},{7,6},{8,9},{9,8},{10,11... | collective-permute-start | bytes 589832 | tf_op jit(solution)/shard_map/ppermute | solution.py:31
  54.9 2.6 %collective-permute-start.3 = (bf16[48,2048]{1,0:T(8,128)(2,1)S(1)}, bf16[48,2048]{1,0:T(8,128)(2,1)}, u32[]{:S(2)}, u32[]{:S(2)}) collective-permute-start(bf16[48,2048]{1,0:T(8,128)(2,1)S(1)} %get-tuple-element.35), channel_id=1, source_target_pairs={{0,2},{1,3},{2,0},{3,1},{4,6},{5,7},{6,4},{7,5},{8,10},{9,11},{10,... | collective-permute-start | bytes 589832 | tf_op jit(solution)/shard_map/ppermute | solution.py:31
  57.7 1.4 %slice_bitcast_fusion = (f32[1,2048,128]{2,1,0:T(8,128)}, f32[1,2048,128]{2,1,0:T(8,128)}) fusion(f32[2048,256]{1,0:T(8,128)S(1)} %fusion.42), kind=kLoop, calls=%fused_computation.21 | loop fusion | bytes 4194304 | tf_op jit(solution)/shard_map/broadcast_in_dim | solution.py:154
  59.2 1.6 %reshape.154 = f32[4,12,8192]{2,1,0:T(8,128)S(1)} reshape(f32[48,8192]{1,0:T(8,128)} %get-tuple-element.41) | data formatting | bytes 3145728 | tf_op jit(solution)/shard_map/reshape | solution.py:132
  60.8 3.8 %collective-permute-done.4 = bf16[48,2048]{1,0:T(8,128)(2,1)} collective-permute-done((bf16[48,2048]{1,0:T(8,128)(2,1)S(1)}, bf16[48,2048]{1,0:T(8,128)(2,1)}, u32[]{:S(2)}, u32[]{:S(2)}) %collective-permute-start.4) | collective-permute-done | bytes 196640 | tf_op jit(solution)/shard_map/ppermute | solution.py:31
  64.6 1.1 %reshape.170 = f32[1,12,8192]{2,1,0:T(8,128)S(1)} reshape(bf16[48,2048]{1,0:T(8,128)(2,1)} %collective-permute-done.4) | data formatting | bytes 589824 | tf_op jit(solution)/shard_map/reshape | solution.py:135
  65.6 6.6 %collective-permute-done.3 = bf16[48,2048]{1,0:T(8,128)(2,1)} collective-permute-done((bf16[48,2048]{1,0:T(8,128)(2,1)S(1)}, bf16[48,2048]{1,0:T(8,128)(2,1)}, u32[]{:S(2)}, u32[]{:S(2)}) %collective-permute-start.3) | collective-permute-done | bytes 196640 | tf_op jit(solution)/shard_map/ppermute | solution.py:31
  72.2 1.1 %reshape.168 = f32[1,12,8192]{2,1,0:T(8,128)S(1)} reshape(bf16[48,2048]{1,0:T(8,128)(2,1)} %collective-permute-done.3) | data formatting | bytes 589824 | tf_op jit(solution)/shard_map/reshape | solution.py:135
  73.3 0.9 %reshape.166 = f32[1,12,8192]{2,1,0:T(8,128)} reshape(bf16[48,2048]{1,0:T(8,128)(2,1)S(1)} %collective-permute-done.2) | data formatting | bytes 589824 | tf_op jit(solution)/shard_map/reshape | solution.py:135
  74.2 1.1 %add_add_fusion = f32[1,12,8192]{2,1,0:T(8,128)S(1)} fusion(f32[1,12,8192]{2,1,0:T(8,128)S(1)} %reshape.170, f32[1,12,8192]{2,1,0:T(8,128)S(1)} %reshape.168, f32[1,12,8192]{2,1,0:T(8,128)} %reshape.166, f32[4,12,8192]{2,1,0:T(8,128)S(1)} %reshape.154, s32[]{:T(128)S(6)} %select_n.68), kind=kLoop, calls=%fused_computation.30 | loop fusion | flops 294912 | bytes 1966084 | tf_op jit(solution)/shard_map/add | solution.py:135
  75.3 1.2 %copy.59 = f32[1,12,8192]{2,0,1:T(1,128)} copy(f32[1,12,8192]{2,1,0:T(8,128)S(1)} %add_add_fusion) | data formatting | bytes 786432
  (64 shorter events, 9.3 us)
Async XLA Ops:
  0.6 8.6 %copy-start.6 = (bf16[1,2,256,1024]{3,2,1,0:T(8,128)(2,1)S(1)}, bf16[1,2,256,1024]{3,2,1,0:T(8,128)(2,1)}, u32[]{:S(2)}) copy-start(bf16[1,2,256,1024]{3,2,1,0:T(8,128)(2,1)} %param.7) | copy-start | bytes 3145732
  0.6 23.8 %collective-permute-start = (bf16[48,8192]{1,0:T(8,128)(2,1)}, bf16[48,8192]{1,0:T(8,128)(2,1)}, u32[]{:S(2)}, u32[]{:S(2)}) collective-permute-start(bf16[48,8192]{1,0:T(8,128)(2,1)} %bitcast.121), channel_id=1, source_target_pairs={{0,16},{16,0},{1,17},{17,1},{2,18},{18,2},{3,19},{19,3},{4,20},{20... | collective-permute-start | bytes 2359304 | tf_op jit(solution)/shard_map/ppermute | solution.py:31
  3.4 13.2 %collective-permute-start.5 = (bf16[48,2048]{1,0:T(8,128)(2,1)}, bf16[48,2048]{1,0:T(8,128)(2,1)}, u32[]{:S(2)}, u32[]{:S(2)}) collective-permute-start(bf16[48,2048]{1,0:T(8,128)(2,1)} %get-tuple-element.30), channel_id=1, source_target_pairs={{0,4},{4,0},{8,12},{12,8},{1,5},{5,1},{9,13},{13,9},{2,6},{6,2},{1... | collective-permute-start | bytes 589832 | tf_op jit(solution)/shard_map/ppermute | solution.py:31
  5.9 11.5 %collective-permute-start.6 = (bf16[48,2048]{1,0:T(8,128)(2,1)}, bf16[48,2048]{1,0:T(8,128)(2,1)}, u32[]{:S(2)}, u32[]{:S(2)}) collective-permute-start(bf16[48,2048]{1,0:T(8,128)(2,1)} %get-tuple-element.29), channel_id=1, source_target_pairs={{0,8},{4,12},{8,0},{12,4},{1,9},{5,13},{9,1},{13,5},{2,10},{6,14},... | collective-permute-start | bytes 589832 | tf_op jit(solution)/shard_map/ppermute | solution.py:31
  7.5 9.9 %collective-permute-start.7 = (bf16[48,2048]{1,0:T(8,128)(2,1)}, bf16[48,2048]{1,0:T(8,128)(2,1)}, u32[]{:S(2)}, u32[]{:S(2)}) collective-permute-start(bf16[48,2048]{1,0:T(8,128)(2,1)} %get-tuple-element.28), channel_id=1, source_target_pairs={{0,12},{4,8},{8,4},{12,0},{1,13},{5,9},{9,5},{13,1},{2,14},{6,10},... | collective-permute-start | bytes 589832 | tf_op jit(solution)/shard_map/ppermute | solution.py:31
  10.3 1.9 %copy-start.3 = (bf16[1,8192,128]{2,1,0:T(8,128)(2,1)S(1)}, bf16[1,8192,128]{2,1,0:T(8,128)(2,1)}, u32[]{:S(2)}) copy-start(bf16[1,8192,128]{2,1,0:T(8,128)(2,1)} %param.10) | copy-start | bytes 6291460
  19.6 22.3 %collective-permute-start.8 = (bf16[192,2048]{1,0:T(8,128)(2,1)}, bf16[192,2048]{1,0:T(8,128)(2,1)}, u32[]{:S(2)}, u32[]{:S(2)}) collective-permute-start(bf16[192,2048]{1,0:T(8,128)(2,1)} %pad_maximum_fusion.1), channel_id=1, source_target_pairs={{0,16},{16,0},{1,17},{17,1},{2,18},{18,2},{3,19},{19,3},{4,20},{20... | collective-permute-start | bytes 2359304 | tf_op jit(solution)/shard_map/ppermute | solution.py:31
  24.4 3.6 %copy-start.2 = (bf16[2,256,8,128]{3,2,1,0:T(8,128)(2,1)S(1)}, bf16[2,256,8,128]{3,2,1,0:T(8,128)(2,1)}, u32[]{:S(2)}) copy-start(bf16[2,256,8,128]{3,2,1,0:T(8,128)(2,1)} %fusion.2) | copy-start | bytes 3145732
  28.6 0.9 %copy-start.7 = (f32[2,8,256,48]{2,3,1,0:T(8,128)}, f32[2,8,256,48]{2,3,1,0:T(8,128)S(1)}, u32[]{:S(2)}) copy-start(f32[2,8,256,48]{2,3,1,0:T(8,128)S(1)} %get-tuple-element.39) | copy-start | bytes 2359300
  32.0 8.0 %copy-start.8 = (f32[2,8,256,48]{2,3,1,0:T(8,128)S(1)}, f32[2,8,256,48]{2,3,1,0:T(8,128)}, u32[]{:S(2)}) copy-start(f32[2,8,256,48]{2,3,1,0:T(8,128)} %copy-done.7) | copy-start | bytes 2359300
  32.1 9.8 %collective-permute-start.11 = (bf16[2,48,256]{2,1,0:T(8,128)(2,1)S(1)}, bf16[2,48,256]{2,1,0:T(8,128)(2,1)S(1)}, u32[]{:S(2)}, u32[]{:S(2)}) collective-permute-start(bf16[2,48,256]{2,1,0:T(8,128)(2,1)S(1)} %pad_maximum_fusion.4), channel_id=1, source_target_pairs={{0,12},{4,8},{8,4},{12,0},{1,13},{5,9},{9,5},{13,1},{2,14},{6,10},... | collective-permute-start | bytes 147464 | tf_op jit(solution)/shard_map/ppermute | solution.py:31
  34.2 7.7 %collective-permute-start.10 = (bf16[2,48,256]{2,1,0:T(8,128)(2,1)S(1)}, bf16[2,48,256]{2,1,0:T(8,128)(2,1)S(1)}, u32[]{:S(2)}, u32[]{:S(2)}) collective-permute-start(bf16[2,48,256]{2,1,0:T(8,128)(2,1)S(1)} %pad_maximum_fusion.4), channel_id=1, source_target_pairs={{0,8},{4,12},{8,0},{12,4},{1,9},{5,13},{9,1},{13,5},{2,10},{6,14},... | collective-permute-start | bytes 147464 | tf_op jit(solution)/shard_map/ppermute | solution.py:31
  34.8 7.0 %collective-permute-start.9 = (bf16[2,48,256]{2,1,0:T(8,128)(2,1)S(1)}, bf16[2,48,256]{2,1,0:T(8,128)(2,1)S(1)}, u32[]{:S(2)}, u32[]{:S(2)}) collective-permute-start(bf16[2,48,256]{2,1,0:T(8,128)(2,1)S(1)} %pad_maximum_fusion.4), channel_id=1, source_target_pairs={{0,4},{4,0},{8,12},{12,8},{1,5},{5,1},{9,13},{13,9},{2,6},{6,2},{1... | collective-permute-start | bytes 147464 | tf_op jit(solution)/shard_map/ppermute | solution.py:31
  40.0 1.9 %copy-start = (bf16[384,2048]{1,0:T(8,128)(2,1)S(1)}, bf16[384,2048]{1,0:T(8,128)(2,1)}, u32[]{:S(2)}) copy-start(bf16[384,2048]{1,0:T(8,128)(2,1)} %constant_dynamic-update-slice_fusion.1) | copy-start | bytes 4718596
  40.0 6.5 %collective-permute-start.1 = (bf16[48,8192]{1,0:T(8,128)(2,1)}, bf16[48,8192]{1,0:T(8,128)(2,1)}, u32[]{:S(2)}, u32[]{:S(2)}) collective-permute-start(bf16[48,8192]{1,0:T(8,128)(2,1)} %convolution_convert_fusion), channel_id=1, source_target_pairs={{0,16},{16,0},{1,17},{17,1},{2,18},{18,2},{3,19},{19,3},{4,20},{20... | collective-permute-start | bytes 2359304 | tf_op jit(solution)/shard_map/ppermute | solution.py:31
  43.1 1.2 %copy-start.1 = (bf16[384,2048]{1,0:T(8,128)(2,1)}, bf16[384,2048]{1,0:T(8,128)(2,1)S(1)}, u32[]{:S(2)}) copy-start(bf16[384,2048]{1,0:T(8,128)(2,1)S(1)} %constant_dynamic-update-slice_fusion) | copy-start | bytes 4718596
  44.3 2.3 %copy-start.4 = (bf16[1,8192,128]{2,1,0:T(8,128)(2,1)S(1)}, bf16[1,8192,128]{2,1,0:T(8,128)(2,1)}, u32[]{:S(2)}) copy-start(bf16[1,8192,128]{2,1,0:T(8,128)(2,1)} %param.10) | copy-start | bytes 6291460
  44.3 2.7 %copy-start.5 = (bf16[1,8192,128]{2,1,0:T(8,128)(2,1)S(1)}, bf16[1,8192,128]{2,1,0:T(8,128)(2,1)}, u32[]{:S(2)}) copy-start(bf16[1,8192,128]{2,1,0:T(8,128)(2,1)} %param.9) | copy-start | bytes 6291460
  53.3 11.3 %collective-permute-start.4 = (bf16[48,2048]{1,0:T(8,128)(2,1)S(1)}, bf16[48,2048]{1,0:T(8,128)(2,1)}, u32[]{:S(2)}, u32[]{:S(2)}) collective-permute-start(bf16[48,2048]{1,0:T(8,128)(2,1)S(1)} %get-tuple-element.34), channel_id=1, source_target_pairs={{0,1},{1,0},{2,3},{3,2},{4,5},{5,4},{6,7},{7,6},{8,9},{9,8},{10,11... | collective-permute-start | bytes 589832 | tf_op jit(solution)/shard_map/ppermute | solution.py:31
  54.9 17.2 %collective-permute-start.3 = (bf16[48,2048]{1,0:T(8,128)(2,1)S(1)}, bf16[48,2048]{1,0:T(8,128)(2,1)}, u32[]{:S(2)}, u32[]{:S(2)}) collective-permute-start(bf16[48,2048]{1,0:T(8,128)(2,1)S(1)} %get-tuple-element.35), channel_id=1, source_target_pairs={{0,2},{1,3},{2,0},{3,1},{4,6},{5,7},{6,4},{7,5},{8,10},{9,11},{10,... | collective-permute-start | bytes 589832 | tf_op jit(solution)/shard_map/ppermute | solution.py:31
  57.5 15.7 %collective-permute-start.2 = (bf16[48,2048]{1,0:T(8,128)(2,1)S(1)}, bf16[48,2048]{1,0:T(8,128)(2,1)S(1)}, u32[]{:S(2)}, u32[]{:S(2)}) collective-permute-start(bf16[48,2048]{1,0:T(8,128)(2,1)S(1)} %get-tuple-element.33), channel_id=1, source_target_pairs={{0,3},{1,2},{2,1},{3,0},{4,7},{5,6},{6,5},{7,4},{8,11},{9,10},{10,... | collective-permute-start | bytes 589832 | tf_op jit(solution)/shard_map/ppermute | solution.py:31

commit v2 on v0

v2 whole, which is shorter than its diff:
```python
import functools
import math

import jax
import jax.numpy as jnp
from jax import lax
from jax.experimental import pallas as pl
from jax.experimental.pallas import tpu as pltpu
from jax.sharding import PartitionSpec as P

EPSILON = 1e-06
KERNEL_BYTES = 16 << 20
F32 = jnp.float32
BF16 = jnp.bfloat16
VMEM = pl.BlockSpec(memory_space=pltpu.VMEM)
SMEM = pl.BlockSpec(memory_space=pltpu.SMEM)
NT = (((1,), (1,)), ((), ()))
TN = (((0,), (0,)), ((), ()))


def partner(index, step, size):
    if size & (size - 1) == 0:
        return index ^ step
    return (index + step) % size


def source(index, step, size):
    if size & (size - 1) == 0:
        return index ^ step
    return (index - step) % size


def swap(value, axis, step, size):
    return lax.ppermute(value, axis, [(i, partner(i, step, size)) for i in range(size)])


def cost(flops, moved, transcendentals=0):
    return pl.CostEstimate(flops=flops, bytes_accessed=moved, transcendentals=transcendentals)


def chunk_of(length, largest):
    best = length
    for size in range(128, largest + 1, 128):
        if length % size == 0:
            best = size
    return min(best, length)


def params():
    return pltpu.CompilerParams(vmem_limit_bytes=KERNEL_BYTES)


def norm_kernel(hd, q_ref, qn_ref):

    for m in range(q_ref.shape[1]):
        for h in range(q_ref.shape[3] // hd):
            lanes = slice(h * hd, (h + 1) * hd)
            x = q_ref[0, m, :, lanes].astype(F32)
            factor = lax.rsqrt(jnp.mean(x * x, axis=-1, keepdims=True) + EPSILON)
            qn_ref[m, :, lanes] = (x * factor).astype(BF16)


def norm_call(queries, hd):
    return pl.pallas_call(
        functools.partial(norm_kernel, hd),
        in_specs=[VMEM],
        out_specs=VMEM,
        out_shape=jax.ShapeDtypeStruct(queries.shape[1:], BF16),
        cost_estimate=cost(4 * queries.size, 4 * queries.size),
        compiler_params=params(),
        name="norm",
    )(queries)


def packed_rows(rows, columns, width):
    return 16 * -(-(rows // 16) // (columns // width))


def packed_block(t, columns, width):
    side = columns // width
    return slice(t // side * 16, t // side * 16 + 16), slice(t % side * width, (t % side + 1) * width)


def spread(lhs, wk_ref, wv_ref, folds, begin, step):
    columns = wk_ref.shape[0] // folds
    total = None
    for f in range(folds):
        rows = pl.ds(f * columns + begin, step)
        pair = jnp.concatenate([wk_ref[rows, :], wv_ref[rows, :]], axis=1)
        term = lax.dot_general(lhs(f), pair, NT, preferred_element_type=F32)
        total = term if total is None else total + term
    return total


def attend_kernel(sizes, place_ref, masks_ref, lengths_ref, wk_ref, wv_ref, qn_ref, gc_ref, *refs):
    n_seg, n_dp, n_mp, folds, out_rows = sizes
    part_refs, refs = refs[:n_seg], refs[n_seg:]
    grads_ref, weights_ref, values_ref, lhs_ref = refs[:4]
    away_refs, refs = refs[4 : 3 + n_seg], refs[3 + n_seg :]
    message_refs, (proj_ref, order_ref, scratch_ref) = refs[: n_dp - 1], refs[n_dp - 1 :]
    held, width = part_refs[0].shape
    hd = wk_ref.shape[1]
    samples, text = qn_ref.shape[:2]
    part = held // samples
    tokens = part * n_seg
    rows = tokens * samples
    heads = qn_ref.shape[2] // hd
    blocks, tiles = masks_ref.shape[1], masks_ref.shape[2]
    root_scale = 1.0 / math.sqrt(hd)
    seg, dp, mp = place_ref[0], place_ref[1], place_ref[2]

    step = chunk_of(width, 2048)
    total = None
    for begin in range(0, width, step):
        chunk = slice(begin, begin + step)
        lhs = jnp.concatenate([ref[:, chunk] for ref in part_refs], axis=0)
        pair = jnp.concatenate([wk_ref[chunk, :], wv_ref[chunk, :]], axis=1)
        term = jnp.dot(lhs, pair, preferred_element_type=F32)
        total = term if total is None else total + term
    proj_ref[...] = total

    row = lax.broadcasted_iota(jnp.int32, (tokens, text), 0)
    position = lax.broadcasted_iota(jnp.int32, (tokens, text), 1)
    token = jnp.zeros((tokens, text), jnp.int32)
    for r in range(n_seg):
        moved = row - r * part + source(seg, r, n_seg) * part
        token = jnp.where(row // part == r, moved, token)
    for m in range(samples):
        raw = jnp.concatenate(
            [proj_ref[r * held + m * part : r * held + (m + 1) * part, :] for r in range(n_seg)], axis=0
        )
        key_raw = raw[:, :hd]
        key_factor = lax.rsqrt(jnp.mean(key_raw * key_raw, axis=-1, keepdims=True) + EPSILON)
        key_norm = key_raw * key_factor
        keys = key_norm.astype(BF16)
        values = raw[:, hd:].astype(BF16)
        values_ref[m] = values
        allowed = jnp.zeros((tokens, text), F32)
        for block in range(blocks):
            for tile in range(tiles):
                inside = (token // (tokens // tiles) == tile) & (position // (text // blocks) == block)
                allowed = jnp.where(inside & (masks_ref[m, block, tile] == 1), 1.0, allowed)
        allowed = jnp.where(position < lengths_ref[m], allowed, 0.0)
        grad_key_norm = jnp.zeros((tokens, hd), F32)
        grad_values = jnp.zeros((tokens, hd), F32)
        for h in range(heads):
            lanes = slice(h * hd, (h + 1) * hd)
            query = qn_ref[m, :, lanes]
            grads = gc_ref[0, m, :, lanes]
            scores = lax.dot_general(keys, query, NT, preferred_element_type=F32) * root_scale
            exponent = jnp.exp(scores) * allowed
            total = jnp.sum(exponent, axis=0, keepdims=True)
            probability = exponent * (1.0 / jnp.where(total > 0, total, 1.0))
            weights = probability.astype(BF16)
            weights_ref[m, h] = weights
            grad_weights = lax.dot_general(values, grads, NT, preferred_element_type=F32)
            inner = jnp.sum(probability * grad_weights, axis=0, keepdims=True)
            grad_scores = (probability * (grad_weights - inner) * root_scale).astype(BF16)
            grad_key_norm += jnp.dot(grad_scores, query, preferred_element_type=F32)
            grad_values += jnp.dot(weights, grads, preferred_element_type=F32)
        inner = jnp.mean(grad_key_norm * key_norm, axis=-1, keepdims=True)
        grad_keys = key_factor * (grad_key_norm - key_norm * inner)
        for r in range(n_seg):
            here = slice(r * held + m * part, r * held + (m + 1) * part)
            there = slice(r * part, (r + 1) * part)
            order_ref[here, :hd] = grad_keys[there]
            order_ref[here, hd:] = grad_values[there]
    ordered = order_ref[...].astype(BF16)
    grads_ref[...] = ordered

    size = folds * out_rows
    count = n_mp * size
    row = lax.broadcasted_iota(jnp.int32, (count, rows), 0)
    column = lax.broadcasted_iota(jnp.int32, (count, rows), 1)
    peer = row // size
    fold = (row - peer * size) // out_rows
    index = row - peer * size - fold * out_rows
    for r in range(n_seg):
        wanted = partner(seg, r, n_seg) * (rows // n_seg) + partner(mp, peer, n_mp) * out_rows + index
        sample = wanted // tokens
        place = wanted - sample * tokens
        owner = place // part
        wanted = source(seg, owner, n_seg) * held + sample * part + place - owner * part
        target = lhs_ref if r == 0 else scratch_ref
        for f in range(folds):
            chosen = jnp.where((column == wanted) & (fold == f), 1.0, 0.0).astype(BF16)
            target[f] = jnp.dot(chosen, ordered, preferred_element_type=F32).astype(BF16)
        if r > 0:
            columns = width // folds
            step = chunk_of(columns, 1024)
            for begin in range(0, columns, step):
                away_refs[r - 1][:, begin : begin + step] = spread(
                    lambda f: scratch_ref[f], wk_ref, wv_ref, folds, begin, step
                ).astype(BF16)

    columns = width // n_dp
    top = packed_rows(rows, columns, 2 * hd)
    for k, message_ref in enumerate(message_refs, 1):
        begin = pl.multiple_of(partner(dp, k, n_dp) * columns, 128)
        message_ref[top:, :] = part_refs[0][:, pl.ds(begin, columns)]
        for t in range(rows // 16):
            down, along = packed_block(t, columns, 2 * hd)
            message_ref[down, along] = ordered[t * 16 : (t + 1) * 16]


def attend_call(sizes, place, masks, lengths, wk, wv, qn, gc, parts):
    n_seg, n_dp, n_mp, folds, out_rows = sizes
    held, width = parts[0].shape
    hd = wk.shape[1]
    samples, text = qn.shape[:2]
    heads = qn.shape[2] // hd
    tokens = held // samples * n_seg
    rows = held * n_seg
    count = n_mp * folds * out_rows
    columns = width // n_dp
    top = packed_rows(rows, columns, 2 * hd)
    shape = jax.ShapeDtypeStruct
    return pl.pallas_call(
        functools.partial(attend_kernel, sizes),
        in_specs=[SMEM] * 3 + [VMEM] * (4 + n_seg),
        out_specs=[VMEM] * (3 + n_seg + n_dp - 1),
        out_shape=[
            shape((rows, 2 * hd), BF16),
            shape((samples, heads, tokens, text), BF16),
            shape((samples, tokens, hd), BF16),
            shape((folds, count, 2 * hd), BF16),
        ]
        + [shape((count, width // folds), BF16)] * (n_seg - 1)
        + [shape((top + held, columns), BF16)] * (n_dp - 1),
        scratch_shapes=[
            pltpu.VMEM((rows, 2 * hd), F32),
            pltpu.VMEM((rows, 2 * hd), F32),
            pltpu.VMEM((folds, count, 2 * hd), BF16),
        ],
        cost_estimate=cost(8 * rows * width * hd + 8 * qn.size * tokens, 4 * wk.size + 8 * qn.size),
        compiler_params=params(),
        name="attend",
    )(place, masks, lengths, wk, wv, qn, gc, *parts)


def context_kernel(weights_ref, values_ref, out_ref):
    samples, heads = weights_ref.shape[:2]
    hd = values_ref.shape[2]
    for m in range(samples):
        for h in range(heads):
            product = lax.dot_general(
                weights_ref[m, h], values_ref[m], TN, preferred_element_type=F32
            )
            out_ref[0, m, :, h * hd : (h + 1) * hd] = product.astype(BF16)


def context_call(weights, values):
    samples, heads, tokens, text = weights.shape
    hd = values.shape[2]
    return pl.pallas_call(
        context_kernel,
        in_specs=[VMEM, VMEM],
        out_specs=VMEM,
        out_shape=jax.ShapeDtypeStruct((1, samples, text, heads * hd), BF16),
        cost_estimate=cost(2 * weights.size * hd, 2 * weights.size + 2 * samples * text * heads * hd),
        compiler_params=params(),
        name="context",
    )(weights, values)


def spread_kernel(n_mp, added, lhs_ref, wk_ref, wv_ref, *refs):
    folds = lhs_ref.shape[0]
    added_refs, outs = refs[:added], refs[added:]
    columns = wk_ref.shape[0] // folds
    size = lhs_ref.shape[1] // n_mp
    step = chunk_of(columns, 1024)
    for begin in range(0, columns, step):
        chunk = slice(begin, begin + step)
        total = spread(lambda f: lhs_ref[f], wk_ref, wv_ref, folds, begin, step)
        for other in added_refs:
            total = total + other[:, chunk].astype(F32)
        for k, out in enumerate(outs):
            out[:, chunk] = total[k * size : (k + 1) * size].astype(out.dtype)


def spread_call(lhs, wk, wv, added, n_mp):
    folds, rows, depth = lhs.shape
    width, hd = wk.shape
    columns = width // folds
    return pl.pallas_call(
        functools.partial(spread_kernel, n_mp, len(added)),
        in_specs=[VMEM] * (3 + len(added)),
        out_specs=[VMEM] * n_mp,
        out_shape=[
            jax.ShapeDtypeStruct((rows // n_mp, columns), BF16 if k else F32) for k in range(n_mp)
        ],
        cost_estimate=cost(4 * rows * width * hd, 4 * wk.size + 2 * rows * columns),
        compiler_params=params(),
        name="spread",
    )(lhs, wk, wv, *added)


def finish_kernel(*refs):
    out_ref = refs[-1]
    total = refs[0][...]
    for ref in refs[1:-1]:
        total = total + ref[...].astype(F32)
    size, columns = out_ref.shape[1], total.shape[1]
    for f in range(total.shape[0] // size):
        out_ref[0, :, f * columns : (f + 1) * columns] = total[f * size : (f + 1) * size]


def finish_call(own, others, size):
    rows, columns = own.shape
    width = rows * columns // size
    return pl.pallas_call(
        finish_kernel,
        in_specs=[VMEM] * (1 + len(others)),
        out_specs=VMEM,
        out_shape=jax.ShapeDtypeStruct((1, size, width), F32),
        cost_estimate=cost(4 * own.size, 8 * own.size + 2 * own.size * len(others)),
        compiler_params=params(),
        name="finish",
    )(own, *others)


def weight_kernel(n_seg, n_dp, place_ref, grads_ref, *refs):
    part_refs, message_refs, (gk_ref, gv_ref) = refs[:n_seg], refs[n_seg:-2], refs[-2:]
    rows, width = grads_ref.shape
    hd = width // 2
    held = part_refs[0].shape[0]
    columns = gk_ref.shape[1]
    top = packed_rows(rows, columns, width)
    dp = place_ref[1]
    per = n_dp - 1
    grads = [grads_ref[...]]
    for ref in message_refs[:per]:
        blocks = [packed_block(t, columns, width) for t in range(rows // 16)]
        grads.append(jnp.concatenate([ref[down, along] for down, along in blocks], axis=0))
    stacked = jnp.concatenate(
        [grads[k][r * held : (r + 1) * held] for r in range(n_seg) for k in range(n_dp)], axis=0
    )
    step = chunk_of(columns, 512)
    for begin in range(0, columns, step):
        tokens = []
        for r in range(n_seg):
            first = pl.multiple_of(dp * columns + begin, 128)
            tokens.append(part_refs[r][:, pl.ds(first, step)])
            for k in range(per):
                tokens.append(message_refs[r * per + k][top:, begin : begin + step])
        product = lax.dot_general(
            jnp.concatenate(tokens, axis=0), stacked, TN, preferred_element_type=F32
        )
        gk_ref[0, begin : begin + step, :] = product[:, :hd]
        gv_ref[0, begin : begin + step, :] = product[:, hd:]


def weight_call(n_seg, n_dp, place, grads, parts, messages):
    rows, width = grads.shape
    columns = parts[0].shape[1] // n_dp
    hd = width // 2
    return pl.pallas_call(
        functools.partial(weight_kernel, n_seg, n_dp),
        in_specs=[SMEM] + [VMEM] * (1 + len(parts) + len(messages)),
        out_specs=[VMEM] * 2,
        out_shape=[jax.ShapeDtypeStruct((1, columns, hd), F32)] * 2,
        cost_estimate=cost(
            2 * n_dp * rows * columns * width, 2 * n_dp * rows * columns + 8 * columns * hd
        ),
        compiler_params=params(),
        name="weight",
    )(place, grads, *parts, *messages)


def build(mesh):
    n_seg, n_dp, n_mp = (mesh.shape[name] for name in ("segment", "dp", "mp"))

    def per_device(queries, vision, w_key, w_value, masks, lengths, grad_context):
        samples, part, width = vision.shape
        rows = samples * part * n_seg
        wk, wv = w_key[0], w_value[0]
        out_rows = rows // (n_seg * n_mp)
        folds = 8 // math.gcd(out_rows, 8)
        sizes = (n_seg, n_dp, n_mp, folds, out_rows)
        place = jnp.stack([lax.axis_index(name) for name in ("segment", "dp", "mp")]).astype(jnp.int32)
        own = vision.reshape(samples * part, width)
        parts = [own] + [swap(own, "segment", r, n_seg) for r in range(1, n_seg)]
        qn = norm_call(queries, wk.shape[1])
        outs = attend_call(sizes, place, masks, lengths, wk, wv, qn, grad_context, parts)
        grads, weights, values, lhs = outs[:4]
        away = [swap(outs[3 + r], "segment", r, n_seg) for r in range(1, n_seg)]
        messages = outs[3 + n_seg :]
        messages = [swap(messages[k - 1], "dp", k, n_dp) for k in range(1, n_dp)]
        totals = spread_call(lhs, wk, wv, away, n_mp)
        arrived = [swap(totals[k], "mp", k, n_mp) for k in reversed(range(1, n_mp))]
        context = context_call(weights, values)
        crossed = [swap(piece, "segment", r, n_seg) for r in range(1, n_seg) for piece in messages]
        grad_wk, grad_wv = weight_call(n_seg, n_dp, place, grads, parts, messages + crossed)
        grad_vision = finish_call(totals[0], arrived, out_rows)
        return (context, grad_vision, grad_wk, grad_wv)

    return per_device


def solution(mesh):
    in_specs = (
        P("segment", "dp", None, "mp"),
        P("dp", "segment", None),
        P("segment", None, "mp"),
        P("segment", None, "mp"),
        P("dp", None, None),
        P("dp"),
        P("segment", "dp", None, "mp"),
    )
    out_specs = (
        P("segment", "dp", None, "mp"),
        P("dp", ("segment", "mp"), None),
        P("segment", "dp", "mp"),
        P("segment", "dp", "mp"),
    )
    return jax.shard_map(
        build(mesh), mesh=mesh, in_specs=in_specs, out_specs=out_specs, check_vma=False
    )
```

time: 176 us -> 55.1 us (0.31)
  the two profiles are of different devices: /device:TPU:24 before, /device:TPU:0 now
where the time goes in v2:
time: 55.1 us; the launch traced here: 54.9 us
  waiting for transfers between devices  24.5 us (44%)
  Pallas kernels  13.1 us (24%)
  starting transfers between devices  10.1 us (18%)
  local copies, waits for them, and re-layouts  6.39 us (12%)
  between operations  0.69 us (1%)
    ppermute x11, waiting for transfers between devices, swap(): lax.ppermute(value, axis, [(i, partner(i, step, size)) for i in range(siz...  24.5 us
    ppermute x11, starting transfers between devices, swap(): lax.ppermute(value, axis, [(i, partner(i, step, size)) for i in range(siz...  10.1 us
    pallas_call x1, Pallas kernels, attend_call(): pl.pallas_call(functools.partial(attend_kernel, sizes), in_specs=[SMEM] *...  6.86 us
    unnamed x15, local copies, waits for them, and re-layouts  6.39 us
    pallas_call x1, Pallas kernels, weight_call(): pl.pallas_call(functools.partial(weight_kernel, n_seg, n_dp), in_specs=[S...  2.63 us
    pallas_call x1, Pallas kernels, context_call(): pl.pallas_call(context_kernel, in_specs=[VMEM, VMEM], out_specs=VMEM, out...  1.46 us
    pallas_call x1, Pallas kernels, spread_call(): pl.pallas_call(functools.partial(spread_kernel, n_mp, len(added)), in_spe...  1.43 us
  transfers between devices with their start and end apart: 11, of which 5 were waited for; matrix products, arithmetic and copies ran while one was open for 0% of the time, Pallas kernels for 11%

profile of v2, /device:TPU:0, one launch (start us, length us, event | category | flops | bytes accessed | tf_op | source)
XLA Modules:
  0.0 54.9 jit_solution(16099801023792352174)
XLA Ops:
  0.6 0.6 %collective-permute-start = (bf16[48,8192]{1,0:T(8,128)(2,1)}, bf16[48,8192]{1,0:T(8,128)(2,1)S(1)}, u32[]{:S(2)}, u32[]{:S(2)}) collective-permute-start(bf16[48,8192]{1,0:T(8,128)(2,1)} %bitcast.10), channel_id=1, source_target_pairs={{0,16},{16,0},{1,17},{17,1},{2,18},{18,2},{3,19},{19,3},{4,20},{20... | collective-permute-start | bytes 2359304 | tf_op jit(solution)/shard_map/ppermute | solution.py:34
  1.2 1.3 %copy-done.4 = bf16[1,2,256,1024]{3,2,1,0:T(8,128)(2,1)S(1)} copy-done((bf16[1,2,256,1024]{3,2,1,0:T(8,128)(2,1)S(1)}, bf16[1,2,256,1024]{3,2,1,0:T(8,128)(2,1)}, u32[]{:S(2)}) %copy-start.4) | copy-done | bytes 1048600
  2.5 0.6 %norm.1.qn_ref = bf16[2,256,1024]{2,1,0:T(8,128)(2,1)S(1)} custom-call(bf16[1,2,256,1024]{3,2,1,0:T(8,128)(2,1)S(1)} %copy-done.4), custom_call_target="tpu_custom_call" | custom-call | flops 2097152 | bytes 2097152 | tf_op jit(solution)/shard_map/norm/pallas_call | solution.py:64
  3.1 0.1 pad_add_fusion.place_ref
  3.2 0.1 collective-permute-done.refs_1_
  3.3 1.6 %copy-done.1 = bf16[1,8192,128]{2,1,0:T(8,128)(2,1)S(1)} copy-done((bf16[1,8192,128]{2,1,0:T(8,128)(2,1)S(1)}, bf16[1,8192,128]{2,1,0:T(8,128)(2,1)}, u32[]{:S(2)}) %copy-start.1) | copy-done | bytes 2097176
  4.9 1.1 %copy-done.2 = bf16[2,24,8192]{2,1,0:T(8,128)(2,1)S(1)} copy-done((bf16[2,24,8192]{2,1,0:T(8,128)(2,1)S(1)}, bf16[2,24,8192]{2,1,0:T(8,128)(2,1)}, u32[]{:S(2)}) %copy-start.2) | copy-done | bytes 786456
  6.1 1.2 %copy-done.3 = bf16[1,2,256,1024]{3,2,1,0:T(8,128)(2,1)S(1)} copy-done((bf16[1,2,256,1024]{3,2,1,0:T(8,128)(2,1)S(1)}, bf16[1,2,256,1024]{3,2,1,0:T(8,128)(2,1)}, u32[]{:S(2)}) %copy-start.3) | copy-done | bytes 1048600
  7.3 6.9 %attend.1 = (bf16[96,256]{1,0:T(8,128)(2,1)S(1)}, bf16[2,8,48,256]{3,2,1,0:T(8,128)(2,1)S(1)}, bf16[2,48,128]{2,1,0:T(8,128)(2,1)S(1)}, bf16[2,96,256]{2,1,0:T(8...) custom-call(s32[3]{0:T(128)S(1)} %pad_add_fusion.place_ref, ...), custom_call_target="tpu_custom_call" | custom-call | flops 1006632960 | bytes 8388608 | tf_op jit(solution)/shard_map/attend/pallas_call | solution.py:218
  14.1 0.4 collective-permute-start.1
  14.6 2.6 %collective-permute-start.5 = (bf16[64,2048]{1,0:T(8,128)(2,1)S(1)}, bf16[64,2048]{1,0:T(8,128)(2,1)S(1)}, u32[]{:S(2)}, u32[]{:S(2)}) collective-permute-start(bf16[64,2048]{1,0:T(8,128)(2,1)S(1)} %get-tuple-element.27), channel_id=1, source_target_pairs={{0,4},{4,0},{8,12},{12,8},{1,5},{5,1},{9,13},{13,9},{2,6},{6,2},{1... | collective-permute-start | bytes 786440 | tf_op jit(solution)/shard_map/ppermute | solution.py:34
  17.2 1.5 %collective-permute-start.6 = (bf16[64,2048]{1,0:T(8,128)(2,1)S(1)}, bf16[64,2048]{1,0:T(8,128)(2,1)S(1)}, u32[]{:S(2)}, u32[]{:S(2)}) collective-permute-start(bf16[64,2048]{1,0:T(8,128)(2,1)S(1)} %get-tuple-element.28), channel_id=1, source_target_pairs={{0,8},{4,12},{8,0},{12,4},{1,9},{5,13},{9,1},{13,5},{2,10},{6,14},... | collective-permute-start | bytes 786440 | tf_op jit(solution)/shard_map/ppermute | solution.py:34
  18.7 0.0 collective-permute-start.7
  18.7 5.6 %collective-permute-done.5.refs_2_ = bf16[64,2048]{1,0:T(8,128)(2,1)S(1)} collective-permute-done((bf16[64,2048]{1,0:T(8,128)(2,1)S(1)}, bf16[64,2048]{1,0:T(8,128)(2,1)S(1)}, u32[]{:S(2)}, u32[]{:S(2)}) %collective-permute-start.5) | collective-permute-done | bytes 262176 | tf_op jit(solution)/shard_map/ppermute | solution.py:34
  24.3 0.0 collective-permute-start.8
  24.3 6.8 %collective-permute-done.6.refs_3_ = bf16[64,2048]{1,0:T(8,128)(2,1)S(1)} collective-permute-done((bf16[64,2048]{1,0:T(8,128)(2,1)S(1)}, bf16[64,2048]{1,0:T(8,128)(2,1)S(1)}, u32[]{:S(2)}, u32[]{:S(2)}) %collective-permute-start.6) | collective-permute-done | bytes 262176 | tf_op jit(solution)/shard_map/ppermute | solution.py:34
  31.1 0.0 collective-permute-start.9
  31.1 0.0 collective-permute-done.7.refs_4_
  31.1 0.5 collective-permute-start.10
  31.6 0.0 collective-permute-done.1.refs_0_
  31.6 1.4 %spread.1 = (f32[24,4096]{1,0:T(8,128)S(1)}, bf16[24,4096]{1,0:T(8,128)(2,1)S(1)}, bf16[24,4096]{1,0:T(8,128)(2,1)S(1)}, bf16[24,4096]{1,0:T(8,128)(2,1)S(1)}) custom-call(bf16[2,96,256]{2,1,0:T(8,128)(2,1)S(1)} %get-tuple-element.20.lhs_ref, bf16[8192,128]{1,0:T(8,128)(2,1)S(1)} %bitcast.7, bf16[8192,128]{1,0:T(8,128)(2,1)S(1)} %bitcast.9, ...), custom_call_target="tpu_custom_call" | custom-call | flops 402653184 | bytes 4980736 | tf_op jit(solution)/shard_map/spread/pallas_call | solution.py:285
  33.1 3.7 %collective-permute-start.2 = (bf16[24,4096]{1,0:T(8,128)(2,1)S(1)}, bf16[24,4096]{1,0:T(8,128)(2,1)S(1)}, u32[]{:S(2)}, u32[]{:S(2)}) collective-permute-start(bf16[24,4096]{1,0:T(8,128)(2,1)S(1)} %get-tuple-element.23), channel_id=1, source_target_pairs={{0,3},{1,2},{2,1},{3,0},{4,7},{5,6},{6,5},{7,4},{8,11},{9,10},{10,... | collective-permute-start | bytes 589832 | tf_op jit(solution)/shard_map/ppermute | solution.py:34
  36.7 0.0 collective-permute-start.3
  36.7 0.8 %collective-permute-start.4 = (bf16[24,4096]{1,0:T(8,128)(2,1)S(1)}, bf16[24,4096]{1,0:T(8,128)(2,1)S(1)}, u32[]{:S(2)}, u32[]{:S(2)}) collective-permute-start(bf16[24,4096]{1,0:T(8,128)(2,1)S(1)} %get-tuple-element.25), channel_id=1, source_target_pairs={{0,1},{1,0},{2,3},{3,2},{4,5},{5,4},{6,7},{7,6},{8,9},{9,8},{10,11... | collective-permute-start | bytes 589832 | tf_op jit(solution)/shard_map/ppermute | solution.py:34
  37.5 1.5 %context.1 = bf16[1,2,256,1024]{3,2,1,0:T(8,128)(2,1)} custom-call(bf16[2,8,48,256]{3,2,1,0:T(8,128)(2,1)S(1)} %get-tuple-element.18.weights_ref, bf16[2,48,128]{2,1,0:T(8,128)(2,1)S(1)} %get-tuple-element.19.values_ref), custom_call_target="tpu_custom_call" | custom-call | flops 50331648 | bytes 1441792 | tf_op jit(solution)/shard_map/context/pallas_call | solution.py:255
  39.0 0.0 collective-permute-done.10.refs_7_
  39.0 2.6 %weight.1 = (f32[1,2048,128]{2,1,0:T(8,128)}, f32[1,2048,128]{2,1,0:T(8,128)}) custom-call(s32[3]{0:T(128)S(1)} %pad_add_fusion.place_ref, bf16[96,256]{1,0:T(8,128)(2,1)S(1)} %get-tuple-element.26.grads_ref, bf16[48,8192]{1,0:T(8,128)(2,1)S(1)} %bitcast.12, bf16[48,8192]{1,0:T(8,128)(2,1)S(1)} %collective-permute-done.refs_1_, ...), custom_call_target="tpu_custom_call" | custom-call | flops 402653184 | bytes 3670016 | tf_op jit(solution)/shard_map/weight/pallas_call | solution.py:357
  41.6 1.2 %collective-permute-done.2.refs_1_ = bf16[24,4096]{1,0:T(8,128)(2,1)S(1)} collective-permute-done((bf16[24,4096]{1,0:T(8,128)(2,1)S(1)}, bf16[24,4096]{1,0:T(8,128)(2,1)S(1)}, u32[]{:S(2)}, u32[]{:S(2)}) %collective-permute-start.2) | collective-permute-done | bytes 196640 | tf_op jit(solution)/shard_map/ppermute | solution.py:34
  42.8 10.7 %collective-permute-done.3.refs_2_ = bf16[24,4096]{1,0:T(8,128)(2,1)S(1)} collective-permute-done((bf16[24,4096]{1,0:T(8,128)(2,1)S(1)}, bf16[24,4096]{1,0:T(8,128)(2,1)S(1)}, u32[]{:S(2)}, u32[]{:S(2)}) %collective-permute-start.3) | collective-permute-done | bytes 196640 | tf_op jit(solution)/shard_map/ppermute | solution.py:34
  53.6 0.0 collective-permute-done.4.refs_3_
  53.6 0.1 finish.1
  53.7 1.2 %copy.11 = f32[1,12,8192]{2,0,1:T(1,128)} copy(f32[1,12,8192]{2,1,0:T(8,128)S(1)} %finish.1) | data formatting | bytes 786432
  (12 shorter events, 0.0 us)
Async XLA Ops:
  0.6 2.7 %copy-start = (bf16[1,8192,128]{2,1,0:T(8,128)(2,1)S(1)}, bf16[1,8192,128]{2,1,0:T(8,128)(2,1)}, u32[]{:S(2)}) copy-start(bf16[1,8192,128]{2,1,0:T(8,128)(2,1)} %param.9) | copy-start | bytes 6291460
  0.6 2.7 %collective-permute-start = (bf16[48,8192]{1,0:T(8,128)(2,1)}, bf16[48,8192]{1,0:T(8,128)(2,1)S(1)}, u32[]{:S(2)}, u32[]{:S(2)}) collective-permute-start(bf16[48,8192]{1,0:T(8,128)(2,1)} %bitcast.10), channel_id=1, source_target_pairs={{0,16},{16,0},{1,17},{17,1},{2,18},{18,2},{3,19},{19,3},{4,20},{20... | collective-permute-start | bytes 2359304 | tf_op jit(solution)/shard_map/ppermute | solution.py:34
  1.2 1.3 %copy-start.4 = (bf16[1,2,256,1024]{3,2,1,0:T(8,128)(2,1)S(1)}, bf16[1,2,256,1024]{3,2,1,0:T(8,128)(2,1)}, u32[]{:S(2)}) copy-start(bf16[1,2,256,1024]{3,2,1,0:T(8,128)(2,1)} %q_ref.1) | copy-start | bytes 3145732
  2.5 0.8 %copy-start.5 = (s32[2,2,2]{2,1,0:T(2,128)S(1)}, s32[2,2,2]{2,1,0:T(2,128)}, u32[]{:S(2)}) copy-start(s32[2,2,2]{2,1,0:T(2,128)} %masks_ref.1) | copy-start | bytes 100
  2.5 0.8 %copy-start.6 = (s32[2]{0:T(128)S(1)}, s32[2]{0:T(128)}, u32[]{:S(2)}) copy-start(s32[2]{0:T(128)} %lengths_ref.1) | copy-start | bytes 28
  3.3 1.6 %copy-start.1 = (bf16[1,8192,128]{2,1,0:T(8,128)(2,1)S(1)}, bf16[1,8192,128]{2,1,0:T(8,128)(2,1)}, u32[]{:S(2)}) copy-start(bf16[1,8192,128]{2,1,0:T(8,128)(2,1)} %param.10) | copy-start | bytes 6291460
  4.9 1.1 %copy-start.2 = (bf16[2,24,8192]{2,1,0:T(8,128)(2,1)S(1)}, bf16[2,24,8192]{2,1,0:T(8,128)(2,1)}, u32[]{:S(2)}) copy-start(bf16[2,24,8192]{2,1,0:T(8,128)(2,1)} %param.8) | copy-start | bytes 2359300
  6.1 1.2 %copy-start.3 = (bf16[1,2,256,1024]{3,2,1,0:T(8,128)(2,1)S(1)}, bf16[1,2,256,1024]{3,2,1,0:T(8,128)(2,1)}, u32[]{:S(2)}) copy-start(bf16[1,2,256,1024]{3,2,1,0:T(8,128)(2,1)} %gc_ref.1) | copy-start | bytes 3145732
  14.1 17.5 %collective-permute-start.1 = (bf16[96,4096]{1,0:T(8,128)(2,1)S(1)}, bf16[96,4096]{1,0:T(8,128)(2,1)S(1)}, u32[]{:S(2)}, u32[]{:S(2)}) collective-permute-start(bf16[96,4096]{1,0:T(8,128)(2,1)S(1)} %get-tuple-element.21), channel_id=1, source_target_pairs={{0,16},{16,0},{1,17},{17,1},{2,18},{18,2},{3,19},{19,3},{4,20},{20... | collective-permute-start | bytes 2359304 | tf_op jit(solution)/shard_map/ppermute | solution.py:34
  14.6 9.8 %collective-permute-start.5 = (bf16[64,2048]{1,0:T(8,128)(2,1)S(1)}, bf16[64,2048]{1,0:T(8,128)(2,1)S(1)}, u32[]{:S(2)}, u32[]{:S(2)}) collective-permute-start(bf16[64,2048]{1,0:T(8,128)(2,1)S(1)} %get-tuple-element.27), channel_id=1, source_target_pairs={{0,4},{4,0},{8,12},{12,8},{1,5},{5,1},{9,13},{13,9},{2,6},{6,2},{1... | collective-permute-start | bytes 786440 | tf_op jit(solution)/shard_map/ppermute | solution.py:34
  17.2 13.9 %collective-permute-start.6 = (bf16[64,2048]{1,0:T(8,128)(2,1)S(1)}, bf16[64,2048]{1,0:T(8,128)(2,1)S(1)}, u32[]{:S(2)}, u32[]{:S(2)}) collective-permute-start(bf16[64,2048]{1,0:T(8,128)(2,1)S(1)} %get-tuple-element.28), channel_id=1, source_target_pairs={{0,8},{4,12},{8,0},{12,4},{1,9},{5,13},{9,1},{13,5},{2,10},{6,14},... | collective-permute-start | bytes 786440 | tf_op jit(solution)/shard_map/ppermute | solution.py:34
  18.7 12.4 %collective-permute-start.7 = (bf16[64,2048]{1,0:T(8,128)(2,1)S(1)}, bf16[64,2048]{1,0:T(8,128)(2,1)S(1)}, u32[]{:S(2)}, u32[]{:S(2)}) collective-permute-start(bf16[64,2048]{1,0:T(8,128)(2,1)S(1)} %get-tuple-element.29), channel_id=1, source_target_pairs={{0,12},{4,8},{8,4},{12,0},{1,13},{5,9},{9,5},{13,1},{2,14},{6,10},... | collective-permute-start | bytes 786440 | tf_op jit(solution)/shard_map/ppermute | solution.py:34
  24.3 12.4 %collective-permute-start.8 = (bf16[64,2048]{1,0:T(8,128)(2,1)S(1)}, bf16[64,2048]{1,0:T(8,128)(2,1)S(1)}, u32[]{:S(2)}, u32[]{:S(2)}) collective-permute-start(bf16[64,2048]{1,0:T(8,128)(2,1)S(1)} %collective-permute-done.5.refs_2_), channel_id=1, source_target_pairs={{0,16},{16,0},{1,17},{17,1},{2,18},{18,2},{3,19},{19,3},{4,20},{20... | collective-permute-start | bytes 786440 | tf_op jit(solution)/shard_map/ppermute | solution.py:34
  31.1 7.9 %collective-permute-start.9 = (bf16[64,2048]{1,0:T(8,128)(2,1)S(1)}, bf16[64,2048]{1,0:T(8,128)(2,1)S(1)}, u32[]{:S(2)}, u32[]{:S(2)}) collective-permute-start(bf16[64,2048]{1,0:T(8,128)(2,1)S(1)} %collective-permute-done.6.refs_3_), channel_id=1, source_target_pairs={{0,16},{16,0},{1,17},{17,1},{2,18},{18,2},{3,19},{19,3},{4,20},{20... | collective-permute-start | bytes 786440 | tf_op jit(solution)/shard_map/ppermute | solution.py:34
  31.1 7.9 %collective-permute-start.10 = (bf16[64,2048]{1,0:T(8,128)(2,1)S(1)}, bf16[64,2048]{1,0:T(8,128)(2,1)S(1)}, u32[]{:S(2)}, u32[]{:S(2)}) collective-permute-start(bf16[64,2048]{1,0:T(8,128)(2,1)S(1)} %collective-permute-done.7.refs_4_), channel_id=1, source_target_pairs={{0,16},{16,0},{1,17},{17,1},{2,18},{18,2},{3,19},{19,3},{4,20},{20... | collective-permute-start | bytes 786440 | tf_op jit(solution)/shard_map/ppermute | solution.py:34
  33.1 9.8 %collective-permute-start.2 = (bf16[24,4096]{1,0:T(8,128)(2,1)S(1)}, bf16[24,4096]{1,0:T(8,128)(2,1)S(1)}, u32[]{:S(2)}, u32[]{:S(2)}) collective-permute-start(bf16[24,4096]{1,0:T(8,128)(2,1)S(1)} %get-tuple-element.23), channel_id=1, source_target_pairs={{0,3},{1,2},{2,1},{3,0},{4,7},{5,6},{6,5},{7,4},{8,11},{9,10},{10,... | collective-permute-start | bytes 589832 | tf_op jit(solution)/shard_map/ppermute | solution.py:34
  36.7 16.9 %collective-permute-start.3 = (bf16[24,4096]{1,0:T(8,128)(2,1)S(1)}, bf16[24,4096]{1,0:T(8,128)(2,1)S(1)}, u32[]{:S(2)}, u32[]{:S(2)}) collective-permute-start(bf16[24,4096]{1,0:T(8,128)(2,1)S(1)} %get-tuple-element.24), channel_id=1, source_target_pairs={{0,2},{1,3},{2,0},{3,1},{4,6},{5,7},{6,4},{7,5},{8,10},{9,11},{10,... | collective-permute-start | bytes 589832 | tf_op jit(solution)/shard_map/ppermute | solution.py:34
  36.7 16.9 %collective-permute-start.4 = (bf16[24,4096]{1,0:T(8,128)(2,1)S(1)}, bf16[24,4096]{1,0:T(8,128)(2,1)S(1)}, u32[]{:S(2)}, u32[]{:S(2)}) collective-permute-start(bf16[24,4096]{1,0:T(8,128)(2,1)S(1)} %get-tuple-element.25), channel_id=1, source_target_pairs={{0,1},{1,0},{2,3},{3,2},{4,5},{5,4},{6,7},{7,6},{8,9},{9,8},{10,11... | collective-permute-start | bytes 589832 | tf_op jit(solution)/shard_map/ppermute | solution.py:34
